TPU v7x, 768 devices: a whole 4x8x12 slice. The times are simulated.
768 devices in a mesh: grp: 8 (over y_hi, core), tp: 8 (over y_lo, x), seq: 12 (over z).
Axes of the slice: x: 4, y: 8 (y_hi: 4, y_lo: 2; y = y_hi * 2 + y_lo), z: 12, core: 2. Of those that a mesh axis runs over, the one named last changes fastest.
Arguments:
- crops: bfloat16 [8, 12, 576, 1024], P('grp', 'seq', 'tp'), may hold values from -6 to 6
- dout: bfloat16 [8, 12, 576, 1024], P('grp', 'seq', None, 'tp'), may hold values from -0.796875 to 0.796875
- crop_count: int32 [8], P('grp'), may hold values from 4 to 12, as said below
- crop_ids: int32 [8, 12], P('grp'), may hold values from 0 to 11, each once within a row
- seq_slot: int32 [8, 12], P('grp'), may hold values from 0 to 11, as said below
- norm_gain: bfloat16 [1024], replicated, may hold values from 0.099609375 to 1.8984375
- qkv_weight: bfloat16 [3, 1024, 1024], P(None, None, 'tp'), may hold values from -40 to 40
Outputs:
- weight_grad: float32 [3072, 1024], P(('grp', 'seq'), 'tp')
Inputs may be any that keep to these rules, and one draw needn't show every extreme that they name: `crop_count`: some page selects 12 crops. `seq_slot`: distinct within a row; only the first crop_count entries of a row are used. `crop_ids`: only the first crop_count entries of a row are used.
All inputs are finite; a program needn't handle non-finite values.
Results may differ from a plain program's by a relative error of at most 0.0084.
Values may be sent and summed in bfloat16 or wider, within the bound.
No kernel may reach another device: no remote copies, remote signals or barrier semaphores. Data moves between devices by JAX's collectives and lax.ppermute only.
A program may use at most 32 MiB of HBM per device.

v0:
```python
import jax
import jax.numpy as jnp
from jax import lax
from jax.sharding import PartitionSpec as P

HD = 64


def crop_grads(inputs, cotangent, norm_gain, weight):
    crops_here, tok_count, head_cols = cotangent.shape
    head_count = head_cols // HD
    values = inputs.astype(jnp.float32)
    centred = values - jnp.mean(values, axis=-1, keepdims=True)
    spread = jnp.mean(centred * centred, axis=-1, keepdims=True)
    normed = (centred * lax.rsqrt(spread + 1e-05) * norm_gain.astype(jnp.float32)).astype(
        jnp.bfloat16
    )
    projected = jnp.einsum(
        "etd,cdw->cetw", normed, weight, preferred_element_type=jnp.float32
    ).astype(jnp.bfloat16)
    heads_view = projected.reshape(3, crops_here, tok_count, head_count, HD)
    queries = heads_view[0]
    key_rows = heads_view[1]
    value_rows = heads_view[2]
    score_scale = HD ** (-0.5)
    scores = (
        jnp.einsum("eqhd,ekhd->ehqk", queries, key_rows, preferred_element_type=jnp.float32)
        * score_scale
    )
    attention = jax.nn.softmax(scores, axis=-1)
    attention_low = attention.astype(jnp.bfloat16)
    upstream = cotangent.reshape(crops_here, tok_count, head_count, HD)
    grad_values = jnp.einsum(
        "ehqk,eqhd->ekhd", attention_low, upstream, preferred_element_type=jnp.float32
    ).astype(jnp.bfloat16)
    grad_attention = jnp.einsum(
        "eqhd,ekhd->ehqk", upstream, value_rows, preferred_element_type=jnp.float32
    )
    grad_scores = attention * (
        grad_attention - jnp.sum(attention * grad_attention, axis=-1, keepdims=True)
    )
    scaled = (grad_scores * score_scale).astype(jnp.bfloat16)
    grad_queries = jnp.einsum(
        "ehqk,ekhd->eqhd", scaled, key_rows, preferred_element_type=jnp.float32
    ).astype(jnp.bfloat16)
    grad_keys = jnp.einsum(
        "ehqk,eqhd->ekhd", scaled, queries, preferred_element_type=jnp.float32
    ).astype(jnp.bfloat16)
    stacked = jnp.stack([grad_queries, grad_keys, grad_values]).reshape(
        3, crops_here, tok_count, head_cols
    )
    return jnp.einsum("etd,cetw->cdw", normed, stacked, preferred_element_type=jnp.float32)


def body(crops, dout, crop_count, crop_ids, seq_slot, norm_gain, qkv_weight):
    seq_index = lax.axis_index("seq")
    model_width = crops.shape[3]
    slot_local = dout.shape[1]
    head_cols = dout.shape[3]
    most_crops = crop_ids.shape[1]
    rank_range = jnp.arange(most_crops, dtype=jnp.int32)
    is_live = (rank_range < crop_count[0]).astype(jnp.float32)
    choose_crop = (crop_ids[0][:, None] == rank_range[None, :]).astype(jnp.float32) * is_live[
        :, None
    ]
    wanted = seq_index * slot_local + jnp.arange(slot_local, dtype=jnp.int32)
    slot_rows = (seq_slot[0][None, :] == wanted[:, None]).astype(jnp.float32)
    selector = jnp.dot(slot_rows, choose_crop).astype(jnp.bfloat16)
    gathered = jnp.einsum(
        "sc,ctd->std",
        selector,
        lax.all_gather(crops, "seq", axis=1, tiled=True)[0],
        preferred_element_type=jnp.float32,
    )
    cotangent = dout[0]
    local_tokens = gathered.astype(jnp.bfloat16)
    full_crops = lax.all_gather(local_tokens, "tp", axis=1, tiled=True)
    local_grad = crop_grads(full_crops, cotangent, norm_gain, qkv_weight)
    grad_rows = local_grad.reshape(3 * model_width, head_cols)
    return lax.psum_scatter(grad_rows, ("grp", "seq"), scatter_dimension=0, tiled=True)


def solution(mesh):
    in_specs = (
        P("grp", "seq", "tp", None),
        P("grp", "seq", None, "tp"),
        P("grp"),
        P("grp", None),
        P("grp", None),
        P(),
        P(None, None, "tp"),
    )
    out_specs = P(("grp", "seq"), "tp")
    return jax.shard_map(body, mesh=mesh, in_specs=in_specs, out_specs=out_specs, check_vma=False)
```

profile of v0, /device:TPU:2, one launch (start us, length us, event | category | flops | bytes accessed | tf_op | source)
XLA Modules:
  0.0 373.7 jit_solution(4437248464949347894)
XLA Ops:
  6.5 0.0 copy-start
  6.5 0.0 all-gather.4.cloned.1.call-start
  6.5 0.7 all-gather.4.cloned.1.call-update
  7.3 0.0 all-gather.6.cloned.1.call-start
  8.0 69.0 %all-gather.4.cloned.1.call-done = bf16[1,12,72,1024]{3,2,0,1:T(8,128)(2,1)} async-done(((bf16[1,1,72,1024]{3,2,0,1:T(8,128)(2,1)}), bf16[1,12,72,1024]{3,2,0,1:T(8,128)(2,1)}) %all-gather.4.cloned.1.call-update) | async-done | bytes 1769488 | tf_op jit(solution)/shard_map/all_gather | solution.py:72
  77.0 2.8 fusion.14
  79.7 0.7 copy.52
  80.5 0.0 all-gather.6.cloned.1.call-update
  80.5 0.0 reduce-scatter.2.cloned.1.call-start
  80.5 0.0 copy-done.3
  80.6 0.2 copy.36
  80.7 42.5 %all-gather.6.cloned.1.call-done = bf16[576,1024]{1,0:T(8,128)(2,1)} async-done(((bf16[72,1024]{1,0:T(8,128)(2,1)}), bf16[576,1024]{1,0:T(8,128)(2,1)}) %all-gather.6.cloned.1.call-update) | async-done | bytes 1179664 | tf_op jit(solution)/shard_map/all_gather | solution.py:77
  123.2 1.5 convert_reduce_fusion
  124.7 1.7 fusion.11
  126.4 0.0 copy-done
  126.5 2.1 fusion.22
  128.6 0.2 copy.35
  128.8 0.2 copy.34
  128.9 0.2 copy.33
  129.1 2.2 fusion.63
  131.3 2.7 fusion.62
  134.0 2.4 fusion.24
  136.4 5.4 %fusion.28 = bf16[2,64,576]{2,1,0:T(8,128)(2,1)S(1)} fusion(bf16[576,2,64]{0,2,1:T(8,128)(2,1)S(1)} %bitcast.126, f32[2,576,576]{2,1,0:T(8,128)} %fusion.63, f32[2,576,576]{1,2,0:T(8,128)} %get-tuple-element.9, f32[2,576]{1,0:T(2,128)S(1)} %get-tuple-element.8), kind=kOutput, calls=%fused_computation.33 | convolution fusion | flops 89654976 | bytes 5607936 | tf_op jit(solution)/shard_map/ehqk,eqhd->ekhd/dot_general | solution.py:46
  141.8 5.5 %fusion.27 = bf16[2,64,576]{2,1,0:T(8,128)(2,1)S(1)} fusion(bf16[576,2,64]{0,2,1:T(8,128)(2,1)S(1)} %bitcast.128, f32[2,576,576]{2,1,0:T(8,128)} %fusion.63, f32[2,576,576]{1,2,0:T(8,128)} %get-tuple-element.9, f32[2,576]{1,0:T(2,128)S(1)} %get-tuple-element.8), kind=kOutput, calls=%fused_computation.32 | convolution fusion | flops 89654976 | bytes 5607936 | tf_op jit(solution)/shard_map/ehqk,ekhd->eqhd/dot_general | solution.py:43
  147.4 0.8 copy.42
  148.1 0.8 copy.40
  148.9 0.8 copy.41
  149.7 0.0 copy-done.1
  149.7 2.0 convolution_bitcast_fusion
  151.7 1.6 copy.43
  153.3 0.0 reduce-scatter.2.cloned.1.call-update
  153.4 213.8 %reduce-scatter.2.cloned.1.call-done = f32[32,128]{1,0:T(8,128)} async-done(((f32[3072,128]{1,0:T(8,128)}), f32[32,128]{1,0:T(8,128)}) %reduce-scatter.2.cloned.1.call-update) | async-done | bytes 16400 | tf_op jit(solution)/shard_map/reduce_scatter | solution.py:80
  (9 shorter events, 0.1 us)
Async XLA Ops:
  6.5 119.9 %copy-start = (bf16[3,1024,128]{2,1,0:T(8,128)(2,1)S(1)}, bf16[3,1024,128]{2,1,0:T(8,128)(2,1)}, u32[]{:S(2)}) copy-start(bf16[3,1024,128]{2,1,0:T(8,128)(2,1)} %param.13) | copy-start | bytes 2359300
  6.5 74.0 %copy-start.3 = (bf16[1024]{0:T(1024)(128)(2,1)S(1)}, bf16[1024]{0:T(1024)(128)(2,1)}, u32[]{:S(2)}) copy-start(bf16[1024]{0:T(1024)(128)(2,1)} %param.12) | copy-start | bytes 6148
  6.5 74.0 %copy-start.2 = (bf16[1,1,576,128]{3,2,1,0:T(8,128)(2,1)S(1)}, bf16[1,1,576,128]{3,2,1,0:T(8,128)(2,1)}, u32[]{:S(2)}) copy-start(bf16[1,1,576,128]{3,2,1,0:T(8,128)(2,1)} %param.8) | copy-start | bytes 442372
  6.5 70.4 %all-gather.4.cloned.1.call-start = ((), (), s32[]{:S(2)}) async-start(), calls=%async_computation.1 | async-start | bytes 1916928 | tf_op jit(solution)/shard_map/all_gather | solution.py:72
  7.3 115.9 %all-gather.6.cloned.1.call-start = ((), (), s32[]{:S(2)}) async-start(), calls=%async_computation.3 | async-start | bytes 1327104 | tf_op jit(solution)/shard_map/all_gather | solution.py:77
  80.5 286.7 %reduce-scatter.2.cloned.1.call-start = ((), (), s32[]{:S(2)}) async-start(), calls=%async_computation.2 | async-start | bytes 1589248 | tf_op jit(solution)/shard_map/reduce_scatter | solution.py:80
  141.8 7.9 %copy-start.1 = (bf16[576,1024]{1,0:T(8,128)(2,1)S(1)}, bf16[576,1024]{1,0:T(8,128)(2,1)}, u32[]{:S(2)}) copy-start(bf16[576,1024]{1,0:T(8,128)(2,1)} %all-gather.6.cloned.1.call-done) | copy-start | bytes 3538948
Sparse Core Ops, SparseCore 0:
  9.7 67.2 all-gather.3
  80.6 42.5 all-gather.5
  153.5 213.6 reduce-scatter.1
where the time goes:
time: 374 us
  waiting for transfers between devices  326 us (87%)
  matrix products  25.1 us (7%)
  between operations  13.9 us (4%)
  local copies, waits for them, and re-layouts  5.39 us (1%)
    reduce_scatter x1, waiting for transfers between devices, body(): lax.psum_scatter(grad_rows, ('grp', 'seq'), scatter_dimension=0, tiled=True)  214 us
    all_gather x1, waiting for transfers between devices, body(): lax.all_gather(crops, 'seq', axis=1, tiled=True)[0]  69 us
    all_gather x1, waiting for transfers between devices, body(): full_crops = lax.all_gather(local_tokens, 'tp', axis=1, tiled=True)  42.5 us
  transfers between devices with their start and end apart: 3, of which 3 were waited for; matrix products, arithmetic and copies ran while one was open for 0% of the time, Pallas kernels for 0%

commit v1 on v0

v1 whole, which is shorter than its diff:
```python
import jax
import jax.numpy as jnp
from jax import lax
from jax.sharding import Mesh, PartitionSpec as P

HD = 64
GRP_OUTER = 4
GRP_INNER = 2


def layer_norm(inputs, norm_gain):
    values = inputs.astype(jnp.float32)
    centred = values - jnp.mean(values, axis=-1, keepdims=True)
    spread = jnp.mean(centred * centred, axis=-1, keepdims=True)
    return (centred * lax.rsqrt(spread + 1e-05) * norm_gain.astype(jnp.float32)).astype(
        jnp.bfloat16
    )


def weight_partials(normed, cotangent, weight):
    tok_count, head_cols = cotangent.shape
    head_count = head_cols // HD
    projected = jnp.einsum(
        "td,cdw->ctw", normed, weight, preferred_element_type=jnp.float32
    ).astype(jnp.bfloat16)
    heads_view = projected.reshape(3, tok_count, head_count, HD)
    queries, key_rows, value_rows = heads_view[0], heads_view[1], heads_view[2]
    score_scale = HD ** (-0.5)
    scores = (
        jnp.einsum("qhd,khd->hqk", queries, key_rows, preferred_element_type=jnp.float32)
        * score_scale
    )
    attention = jax.nn.softmax(scores, axis=-1)
    attention_low = attention.astype(jnp.bfloat16)
    upstream = cotangent.reshape(tok_count, head_count, HD)
    grad_values = jnp.einsum(
        "hqk,qhd->khd", attention_low, upstream, preferred_element_type=jnp.float32
    ).astype(jnp.bfloat16)
    grad_attention = jnp.einsum(
        "qhd,khd->hqk", upstream, value_rows, preferred_element_type=jnp.float32
    )
    grad_scores = attention * (
        grad_attention - jnp.sum(attention * grad_attention, axis=-1, keepdims=True)
    )
    scaled = (grad_scores * score_scale).astype(jnp.bfloat16)
    grad_queries = jnp.einsum(
        "hqk,khd->qhd", scaled, key_rows, preferred_element_type=jnp.float32
    ).astype(jnp.bfloat16)
    grad_keys = jnp.einsum(
        "hqk,qhd->khd", scaled, queries, preferred_element_type=jnp.float32
    ).astype(jnp.bfloat16)
    stacked = jnp.stack([grad_queries, grad_keys, grad_values]).reshape(3, tok_count, head_cols)
    return jnp.einsum("td,ctw->cdw", normed, stacked, preferred_element_type=jnp.float32)


def slot_selector(crop_count, crop_ids, seq_slot):
    most = crop_ids.shape[0]
    numbers = jnp.arange(most, dtype=jnp.int32)
    live = numbers < crop_count
    from_candidate = (crop_ids[None, :] == numbers[:, None]) & live[None, :]
    to_slot = seq_slot[:, None] == numbers[None, :]
    return jnp.dot(from_candidate.astype(jnp.float32), to_slot.astype(jnp.float32))


def make_body(seq_size):
    def body(crops, dout, crop_count, crop_ids, seq_slot, norm_gain, qkv_weight):
        tok_local, width = crops.shape[2:]
        tok_count, head_cols = dout.shape[2:]
        tp_size = tok_count // tok_local
        chunk = tok_count // seq_size

        pieces = lax.all_to_all(
            dout[0, 0].reshape(seq_size, chunk, head_cols), "z", 0, 0, tiled=True
        )
        selector = slot_selector(crop_count[0], crop_ids[0], seq_slot[0]).astype(jnp.bfloat16)
        routed = jnp.einsum(
            "cs,sjw->cjw", selector, pieces, preferred_element_type=jnp.float32
        ).astype(jnp.bfloat16)
        cotangent = lax.all_to_all(routed, "z", 0, 0, tiled=True).reshape(tok_count, head_cols)

        local = layer_norm(crops[0, 0], norm_gain)
        normed = lax.all_to_all(
            jnp.broadcast_to(local[None], (tp_size, tok_local, width)), ("yl", "x"), 0, 0, tiled=True
        ).reshape(tok_count, width)

        partial = weight_partials(normed, cotangent, qkv_weight)

        rows = 3 * width // (GRP_OUTER * GRP_INNER * seq_size)
        core = lax.axis_index("core")
        by_core = partial.reshape(GRP_OUTER, GRP_INNER, seq_size * rows, head_cols)
        theirs = lax.dynamic_index_in_dim(by_core, 1 - core, 1, keepdims=False)
        mine = lax.dynamic_index_in_dim(by_core, core, 1, keepdims=False)
        received = lax.ppermute(theirs.astype(jnp.bfloat16), "core", [(0, 1), (1, 0)])
        total = mine + received.astype(jnp.float32)
        parts = lax.all_to_all(total.astype(jnp.bfloat16), "yh", 0, 0, tiled=True)
        total = jnp.sum(parts.astype(jnp.float32), axis=0)
        parts = lax.all_to_all(
            total.astype(jnp.bfloat16).reshape(seq_size, rows, head_cols), "z", 0, 0, tiled=True
        )
        return jnp.sum(parts.astype(jnp.float32), axis=0)

    return body


def solution(mesh):
    seq_size = mesh.shape["seq"]
    tp_inner = mesh.shape["tp"] // 2
    fine = Mesh(
        mesh.devices.reshape(GRP_OUTER, GRP_INNER, 2, tp_inner, seq_size),
        ("yh", "core", "yl", "x", "z"),
    )
    grp, tp = ("yh", "core"), ("yl", "x")
    in_specs = (
        P(grp, "z", tp, None),
        P(grp, "z", None, tp),
        P(grp),
        P(grp, None),
        P(grp, None),
        P(),
        P(None, None, tp),
    )
    out_specs = P((*grp, "z"), tp)
    return jax.shard_map(
        make_body(seq_size), mesh=fine, in_specs=in_specs, out_specs=out_specs, check_vma=False
    )
```

time: 374 us -> 133 us (0.36)
  the two profiles are of different devices: /device:TPU:2 before, /device:TPU:8 now
where the time goes in v1:
time: 133 us; the launch traced here: 132 us
  waiting for transfers between devices  35 us (26%)
  blocking collectives  34.2 us (26%)
  starting transfers between devices  26.5 us (20%)
  matrix products  21.8 us (16%)
  local copies, waits for them, and re-layouts  7.87 us (6%)
  other arithmetic  5.77 us (4%)
    all_to_all x1, blocking collectives, body(): parts = lax.all_to_all(total.astype(jnp.bfloat16), 'yh', 0, 0, tiled=True)  20 us
    all_to_all x1, starting transfers between devices, body(): lax.all_to_all(dout[0, 0].reshape(seq_size, chunk, head_cols), 'z', 0, 0,...  15.3 us
    all_to_all x1, blocking collectives, body(): lax.all_to_all(total.astype(jnp.bfloat16).reshape(seq_size, rows, head_co...  14.2 us
    all_to_all x1, waiting for transfers between devices, body(): lax.all_to_all(jnp.broadcast_to(local[None], (tp_size, tok_local, width))...  12.7 us
    all_to_all x1, waiting for transfers between devices, body(): lax.all_to_all(routed, 'z', 0, 0, tiled=True).reshape(tok_count, head_cols)  11.3 us
    all_to_all x1, waiting for transfers between devices, body(): lax.all_to_all(dout[0, 0].reshape(seq_size, chunk, head_cols), 'z', 0, 0,...  9.32 us
    all_to_all x1, starting transfers between devices, body(): lax.all_to_all(jnp.broadcast_to(local[None], (tp_size, tok_local, width))...  5.76 us
    dot_general x1, matrix products, weight_partials(): jnp.einsum('hqk,khd->qhd', scaled, key_rows, preferred_element_type=jnp.f...  5.43 us
  transfers between devices with their start and end apart: 4, of which 4 were waited for; matrix products, arithmetic and copies ran while one was open for 3% of the time, Pallas kernels for 0%

profile of v1, /device:TPU:8, one launch (start us, length us, event | category | flops | bytes accessed | tf_op | source)
XLA Modules:
  0.0 131.9 jit_solution(8485365360077534748)
XLA Ops:
  0.0 15.3 %all-to-all-start.1 = ((bf16[12,48,128]{2,1,0:T(8,128)(2,1)}), bf16[12,48,128]{2,1,0:T(8,128)(2,1)S(1)}, u32[]{:S(2)}, u32[]{:S(2)}) async-start(bf16[12,48,128]{2,1,0:T(8,128)(2,1)} %bitcast.75), calls=%async_computation.1 | async-start | bytes 294912 | tf_op jit(solution)/shard_map/all_to_all | solution.py:72
  15.3 1.0 convert_reduce_fusion
  16.3 0.7 convert_element_type.77
  17.7 1.1 fusion.42
  18.8 9.3 %all-to-all-done.1 = bf16[12,48,128]{2,1,0:T(8,128)(2,1)S(1)} async-done(((bf16[12,48,128]{2,1,0:T(8,128)(2,1)}), bf16[12,48,128]{2,1,0:T(8,128)(2,1)S(1)}, u32[]{:S(2)}, u32[]{:S(2)}) %all-to-all-start.1) | async-done | bytes 147488 | tf_op jit(solution)/shard_map/all_to_all | solution.py:72
  28.1 1.0 convolution_convert_fusion.1
  29.2 0.7 copy.50
  29.9 3.5 %all-to-all-start.2 = ((bf16[12,48,128]{2,1,0:T(8,128)(2,1)}), bf16[12,48,128]{2,1,0:T(8,128)(2,1)S(1)}, u32[]{:S(2)}, u32[]{:S(2)}) async-start(bf16[12,48,128]{2,1,0:T(8,128)(2,1)} %copy.50), calls=%async_computation.2 | async-start | bytes 294912 | tf_op jit(solution)/shard_map/all_to_all | solution.py:79
  33.4 1.0 fusion.44
  34.4 11.3 %all-to-all-done.2 = bf16[12,48,128]{2,1,0:T(8,128)(2,1)S(1)} async-done(((bf16[12,48,128]{2,1,0:T(8,128)(2,1)}), bf16[12,48,128]{2,1,0:T(8,128)(2,1)S(1)}, u32[]{:S(2)}, u32[]{:S(2)}) %all-to-all-start.2) | async-done | bytes 147488 | tf_op jit(solution)/shard_map/all_to_all | solution.py:79
  45.7 1.2 broadcast_in_dim.2
  46.9 5.8 %all-to-all-start = ((bf16[8,72,1024]{2,1,0:T(8,128)(2,1)}), bf16[8,72,1024]{2,1,0:T(8,128)(2,1)S(1)}, u32[]{:S(2)}, u32[]{:S(2)}) async-start(bf16[8,72,1024]{2,1,0:T(8,128)(2,1)} %broadcast_in_dim.2), calls=%async_computation | async-start | bytes 2359296 | tf_op jit(solution)/shard_map/all_to_all | solution.py:82
  52.8 0.2 copy.52
  53.0 12.7 %all-to-all-done = bf16[8,72,1024]{2,1,0:T(8,128)(2,1)S(1)} async-done(((bf16[8,72,1024]{2,1,0:T(8,128)(2,1)}), bf16[8,72,1024]{2,1,0:T(8,128)(2,1)S(1)}, u32[]{:S(2)}, u32[]{:S(2)}) %all-to-all-start) | async-done | bytes 1179680 | tf_op jit(solution)/shard_map/all_to_all | solution.py:82
  65.7 0.8 fusion.19
  67.0 2.7 %fusion.62 = (f32[2,576]{1,0:T(2,128)S(1)}, f32[2,576,576]{1,2,0:T(8,128)}) fusion(bf16[576,2,64]{0,2,1:T(8,128)(2,1)S(1)} %bitcast.70, bf16[576,2,64]{0,2,1:T(8,128)(2,1)S(1)} %bitcast.68), kind=kOutput, calls=%fused_computation.61 | convolution fusion | flops 86925888 | bytes 2953728 | tf_op jit(solution)/shard_map/sub | solution.py:33
  69.7 2.2 %fusion.63 = f32[2,576,576]{1,2,0:T(8,128)} fusion(bf16[576,2,64]{0,2,1:T(8,128)(2,1)S(1)} %copy.52, bf16[576,2,64]{0,2,1:T(8,128)(2,1)S(1)} %bitcast.66), kind=kOutput, calls=%fused_computation.62 | convolution fusion | flops 84934656 | bytes 2949120 | tf_op jit(solution)/shard_map/qhd,khd->hqk/dot_general | solution.py:39
  71.9 5.4 %fusion.23 = bf16[2,64,576]{2,1,0:T(8,128)(2,1)S(1)} fusion(bf16[576,2,64]{0,2,1:T(8,128)(2,1)S(1)} %bitcast.69, f32[2,576,576]{1,2,0:T(8,128)} %fusion.63, f32[2,576,576]{1,2,0:T(8,128)} %get-tuple-element.9, f32[2,576]{1,0:T(2,128)S(1)} %get-tuple-element.8), kind=kOutput, calls=%fused_computation.21 | convolution fusion | flops 89654976 | bytes 5607936 | tf_op jit(solution)/shard_map/hqk,khd->qhd/dot_general | solution.py:46
  77.3 5.4 %fusion.26 = bf16[2,64,576]{2,1,0:T(8,128)(2,1)S(1)} fusion(bf16[576,2,64]{0,2,1:T(8,128)(2,1)S(1)} %bitcast.71, f32[2,576,576]{1,2,0:T(8,128)} %fusion.63, f32[2,576,576]{1,2,0:T(8,128)} %get-tuple-element.9, f32[2,576]{1,0:T(2,128)S(1)} %get-tuple-element.8), kind=kOutput, calls=%fused_computation.22 | convolution fusion | flops 89654976 | bytes 5607936 | tf_op jit(solution)/shard_map/hqk,qhd->khd/dot_general | solution.py:49
  82.7 2.4 %fusion.20 = bf16[2,64,576]{2,1,0:T(8,128)(2,1)S(1)} fusion(bf16[576,2,64]{0,2,1:T(8,128)(2,1)S(1)} %copy.52, f32[2,576,576]{1,2,0:T(8,128)} %get-tuple-element.9, f32[2,576]{1,0:T(2,128)S(1)} %get-tuple-element.8), kind=kOutput, calls=%fused_computation.20 | convolution fusion | flops 86335488 | bytes 2953728 | tf_op jit(solution)/shard_map/hqk,qhd->khd/dot_general | solution.py:36
  85.1 0.8 copy.57
  85.9 0.8 copy.58
  86.7 0.8 copy.59
  87.5 1.8 %convolution_bitcast_fusion = f32[3,1024,128]{1,2,0:T(8,128)S(1)} fusion(bf16[576,1024,1]{1,0,2:T(8,128)(2,1)S(1)} %bitcast.65, bf16[1,576,128]{2,1,0:T(8,128)(2,1)} %copy.59, bf16[1,576,128]{2,1,0:T(8,128)(2,1)} %copy.58, bf16[1,576,128]{2,1,0:T(8,128)(2,1)} %copy.57), kind=kOutput, calls=%fused_computation.10 | convolution fusion | flops 453427200 | bytes 3194880 | tf_op jit(solution)/shard_map/td,ctw->cdw/dot_general | solution.py:53
  89.4 1.6 %copy.60 = f32[3,1024,128]{2,1,0:T(8,128)} copy(f32[3,1024,128]{1,2,0:T(8,128)S(1)} %convolution_bitcast_fusion) | data formatting | bytes 3145728 | tf_op jit(solution)/shard_map/td,ctw->cdw/transpose | solution.py:53
  91.0 1.2 fusion.36
  92.2 1.9 %collective-permute-start = (bf16[4,384,128]{2,1,0:T(8,128)(2,1)S(1)}, bf16[4,384,128]{2,1,0:T(8,128)(2,1)S(1)}, u32[]{:S(2)}, u32[]{:S(2)}) collective-permute-start(bf16[4,384,128]{2,1,0:T(8,128)(2,1)S(1)} %fusion.36), channel_id=1, source_target_pairs={{0,96},{96,0},{1,97},{97,1},{2,98},{98,2},{3,99},{99,3},{4,100},{1... | collective-permute-start | bytes 1179656 | tf_op jit(solution)/shard_map/ppermute | solution.py:93
  94.1 1.7 %collective-permute-done = bf16[4,384,128]{2,1,0:T(8,128)(2,1)S(1)} collective-permute-done((bf16[4,384,128]{2,1,0:T(8,128)(2,1)S(1)}, bf16[4,384,128]{2,1,0:T(8,128)(2,1)S(1)}, u32[]{:S(2)}, u32[]{:S(2)}) %collective-permute-start) | collective-permute-done | bytes 393248 | tf_op jit(solution)/shard_map/ppermute | solution.py:93
  95.8 1.2 fusion.30
  97.0 20.0 %all_to_all.25 = bf16[4,384,128]{2,1,0:T(8,128)(2,1)S(1)} all-to-all(bf16[4,384,128]{2,1,0:T(8,128)(2,1)S(1)} %fusion.30), channel_id=1, replica_groups=mesh['yh'=4,'core'=2,'yl'=2,'x'=4,'z'=12] {'yh'}, dimensions={0} | all-to-all | bytes 786432 | tf_op jit(solution)/shard_map/all_to_all | solution.py:95
  117.0 14.2 %all_to_all.26 = bf16[12,32,128]{2,1,0:T(8,128)(2,1)S(1)} all-to-all(bf16[12,32,128]{2,1,0:T(8,128)(2,1)S(1)} %bitcast.67), channel_id=1, replica_groups=mesh['yh'=4,'core'=2,'yl'=2,'x'=4,'z'=12] {'z'}, dimensions={0} | all-to-all | bytes 196608 | tf_op jit(solution)/shard_map/all_to_all | solution.py:97
  131.2 0.6 convert_reduce_fusion.1
  (11 shorter events, 0.7 us)
Async XLA Ops:
  0.0 65.7 %copy-start = (bf16[3,1024,128]{2,1,0:T(8,128)(2,1)S(1)}, bf16[3,1024,128]{2,1,0:T(8,128)(2,1)}, u32[]{:S(2)}) copy-start(bf16[3,1024,128]{2,1,0:T(8,128)(2,1)} %param.13) | copy-start | bytes 2359300
  0.0 28.1 %all-to-all-start.1 = ((bf16[12,48,128]{2,1,0:T(8,128)(2,1)}), bf16[12,48,128]{2,1,0:T(8,128)(2,1)S(1)}, u32[]{:S(2)}, u32[]{:S(2)}) async-start(bf16[12,48,128]{2,1,0:T(8,128)(2,1)} %bitcast.75), calls=%async_computation.1 | async-start | bytes 294912 | tf_op jit(solution)/shard_map/all_to_all | solution.py:72
  29.9 15.8 %all-to-all-start.2 = ((bf16[12,48,128]{2,1,0:T(8,128)(2,1)}), bf16[12,48,128]{2,1,0:T(8,128)(2,1)S(1)}, u32[]{:S(2)}, u32[]{:S(2)}) async-start(bf16[12,48,128]{2,1,0:T(8,128)(2,1)} %copy.50), calls=%async_computation.2 | async-start | bytes 294912 | tf_op jit(solution)/shard_map/all_to_all | solution.py:79
  46.9 18.8 %all-to-all-start = ((bf16[8,72,1024]{2,1,0:T(8,128)(2,1)}), bf16[8,72,1024]{2,1,0:T(8,128)(2,1)S(1)}, u32[]{:S(2)}, u32[]{:S(2)}) async-start(bf16[8,72,1024]{2,1,0:T(8,128)(2,1)} %broadcast_in_dim.2), calls=%async_computation | async-start | bytes 2359296 | tf_op jit(solution)/shard_map/all_to_all | solution.py:82
  92.2 3.6 %collective-permute-start = (bf16[4,384,128]{2,1,0:T(8,128)(2,1)S(1)}, bf16[4,384,128]{2,1,0:T(8,128)(2,1)S(1)}, u32[]{:S(2)}, u32[]{:S(2)}) collective-permute-start(bf16[4,384,128]{2,1,0:T(8,128)(2,1)S(1)} %fusion.36), channel_id=1, source_target_pairs={{0,96},{96,0},{1,97},{97,1},{2,98},{98,2},{3,99},{99,3},{4,100},{1... | collective-permute-start | bytes 1179656 | tf_op jit(solution)/shard_map/ppermute | solution.py:93

commit v2 on v1

v2 whole, which is shorter than its diff:
```python
import jax
import jax.numpy as jnp
from jax import lax
from jax.experimental import pallas as pl
from jax.experimental.pallas import tpu as pltpu
from jax.sharding import Mesh, PartitionSpec as P


HD = 64
GRP_OUTER = 4
GRP_INNER = 2
TP_OUTER = 2

NN = (((1,), (0,)), ((), ()))
NT = (((1,), (1,)), ((), ()))
VMEM = pl.BlockSpec(memory_space=pltpu.VMEM)
SMEM = pl.BlockSpec(memory_space=pltpu.SMEM)
ANY = pl.BlockSpec(memory_space=pl.ANY)


def dot(a, b, dims=NN):
    return lax.dot_general(a, b, dims, preferred_element_type=jnp.float32)


def norm_kernel(inputs_ref, gain_ref, out_ref):
    values = inputs_ref[...].astype(jnp.float32)
    centred = values - jnp.mean(values, axis=-1, keepdims=True)
    spread = jnp.mean(centred * centred, axis=-1, keepdims=True)
    normed = centred * lax.rsqrt(spread + 1e-05) * gain_ref[...].astype(jnp.float32)
    out_ref[...] = normed.astype(jnp.bfloat16)


def layer_norm(inputs, gain):
    return pl.pallas_call(
        norm_kernel,
        out_shape=jax.ShapeDtypeStruct(inputs.shape, jnp.bfloat16),
        in_specs=[VMEM, VMEM],
        out_specs=VMEM,
        name="norm",
    )(inputs, gain)


def route_kernel(count_ref, ids_ref, slot_ref, pieces_hbm, out_ref, pieces_ref, sem):
    copy = pltpu.make_async_copy(pieces_hbm, pieces_ref, sem)
    copy.start()
    out_ref[...] = jnp.zeros(out_ref.shape, out_ref.dtype)
    copy.wait()
    for rank in range(out_ref.shape[0]):

        @pl.when(rank < count_ref[0])
        def _():
            out_ref[ids_ref[0, rank]] = pieces_ref[slot_ref[0, rank]]


def by_candidate(count, ids, slots, pieces):
    return pl.pallas_call(
        route_kernel,
        out_shape=jax.ShapeDtypeStruct(pieces.shape, pieces.dtype),
        in_specs=[SMEM, SMEM, SMEM, ANY],
        out_specs=VMEM,
        scratch_shapes=[pltpu.VMEM(pieces.shape, pieces.dtype), pltpu.SemaphoreType.DMA(())],
        name="route",
    )(count, ids, slots, pieces)


def grads_kernel(place_ref, *refs):
    *block_refs, weight_ref, cotangent_hbm = refs[:-7]
    theirs_ref, mine_ref, sums_ref, blocks_ref, cotangent_ref, block_sems, cotangent_sem = refs[-7:]
    low = jnp.bfloat16
    copies = [
        pltpu.make_async_copy(ref, blocks_ref.at[i], block_sems.at[i])
        for i, ref in enumerate(block_refs)
    ]
    copies.append(pltpu.make_async_copy(cotangent_hbm, cotangent_ref, cotangent_sem))
    for copy in copies:
        copy.start()
    for copy in copies:
        copy.wait()
    normed = jnp.concatenate([blocks_ref[i] for i in range(len(block_refs))], 0)
    tok_count, width = normed.shape
    head_cols = cotangent_ref.shape[1]
    queries = dot(normed, weight_ref[0]).astype(low)
    key_rows = dot(normed, weight_ref[1]).astype(low)
    value_rows = dot(normed, weight_ref[2]).astype(low)
    first = place_ref[1] * blocks_ref.shape[1]
    turn = jnp.where(first == 0, 0, tok_count - first)
    upstream = pltpu.roll(cotangent_ref[...].astype(jnp.float32), turn, 0).astype(low)
    head_of = lax.broadcasted_iota(jnp.int32, (tok_count, head_cols), 1) // HD
    zero = jnp.zeros((), low)
    score_scale = HD ** (-0.5)
    keys_t = key_rows.T
    grad_values, grad_keys, grad_queries = [], [], []
    for head in range(head_cols // HD):
        q = jnp.where(head_of == head, queries, zero)
        g = jnp.where(head_of == head, upstream, zero)
        scores = dot(key_rows, q, NT) * score_scale
        weights = jnp.exp(scores - jnp.max(scores, axis=0, keepdims=True))
        attention = weights / jnp.sum(weights, axis=0, keepdims=True)
        grad_attention = dot(value_rows, g, NT)
        mean = jnp.sum(attention * grad_attention, axis=0, keepdims=True)
        scaled = (attention * (grad_attention - mean) * score_scale).astype(low)
        grad_values.append(dot(attention.astype(low), g))
        grad_keys.append(dot(scaled, q))
        grad_queries.append(dot(keys_t[head * HD : (head + 1) * HD], scaled))
    normed_t = normed.T
    joined = (
        jnp.concatenate(grad_queries, 0).astype(low).T,
        sum(grad_keys).astype(low),
        sum(grad_values).astype(low),
    )
    for c, grad in enumerate(joined):
        sums_ref[pl.ds(c * width, width), :] = dot(normed_t, grad)
    core = place_ref[0]
    seq_size, outer_rows = theirs_ref.shape[:2]
    rows = outer_rows // GRP_OUTER
    for outer in range(GRP_OUTER):
        own = (outer * GRP_INNER + core) * seq_size * rows
        other = (outer * GRP_INNER + 1 - core) * seq_size * rows
        for s in range(seq_size):
            to = pl.ds(outer * rows, rows)
            mine_ref[s, to] = sums_ref[pl.ds(pl.multiple_of(own + s * rows, rows), rows), :]
            theirs_ref[s, to] = sums_ref[
                pl.ds(pl.multiple_of(other + s * rows, rows), rows), :
            ].astype(low)


def weight_partials(place, normed, weight, cotangent, seq_size):
    width, head_cols = weight.shape[1:]
    half = (seq_size, 3 * width // (GRP_INNER * seq_size), head_cols)
    return pl.pallas_call(
        grads_kernel,
        out_shape=(
            jax.ShapeDtypeStruct(half, jnp.bfloat16),
            jax.ShapeDtypeStruct(half, jnp.float32),
        ),
        in_specs=[SMEM, *[ANY] * len(normed), VMEM, ANY],
        out_specs=(VMEM, VMEM),
        scratch_shapes=[
            pltpu.VMEM((3 * width, head_cols), jnp.float32),
            pltpu.VMEM((len(normed), *normed[0].shape), jnp.bfloat16),
            pltpu.VMEM(cotangent.shape, jnp.bfloat16),
            pltpu.SemaphoreType.DMA((len(normed),)),
            pltpu.SemaphoreType.DMA(()),
        ],
        name="grads",
    )(place, *normed, weight, cotangent)


def make_body(seq_size):
    def body(crops, dout, crop_count, crop_ids, seq_slot, norm_gain, qkv_weight):
        return step(crops, dout, crop_count, crop_ids, seq_slot, norm_gain, qkv_weight)

    def step(crops, dout, crop_count, crop_ids, seq_slot, norm_gain, qkv_weight):
        tok_local, _ = crops.shape[2:]
        tok_count, head_cols = dout.shape[2:]
        tp_size = tok_count // tok_local
        chunk = tok_count // seq_size

        pieces = lax.all_to_all(
            dout[0, 0].reshape(seq_size, chunk, head_cols), "z", 0, 0, tiled=True
        )
        routed = by_candidate(crop_count, crop_ids, seq_slot, pieces)
        cotangent = lax.all_to_all(routed, "z", 0, 0, tiled=True)
        cotangent = cotangent.reshape(tok_count, head_cols)

        local = layer_norm(crops[0, 0], norm_gain[None])
        tp = ("yl", "x")
        normed = [local]
        for d in range(1, tp_size):
            pairs = [(i, (i - d) % tp_size) for i in range(tp_size)]
            normed.append(lax.ppermute(local, tp, pairs))

        place = jnp.stack([lax.axis_index("core"), lax.axis_index(tp)])
        theirs, mine = weight_partials(place, normed, qkv_weight, cotangent, seq_size)

        received = lax.ppermute(theirs, "core", [(0, 1), (1, 0)])
        total = mine + received.astype(jnp.float32)
        parts = lax.all_to_all(total.astype(jnp.bfloat16), "z", 0, 0, tiled=True)
        total = jnp.sum(parts.astype(jnp.float32), axis=0)
        parts = lax.all_to_all(
            total.astype(jnp.bfloat16).reshape(GRP_OUTER, -1, head_cols), "yh", 0, 0, tiled=True
        )
        return jnp.sum(parts.astype(jnp.float32), axis=0)

    return body


def solution(mesh):
    seq_size = mesh.shape["seq"]
    tp_inner = mesh.shape["tp"] // TP_OUTER
    fine = Mesh(
        mesh.devices.reshape(GRP_OUTER, GRP_INNER, TP_OUTER, tp_inner, seq_size),
        ("yh", "core", "yl", "x", "z"),
    )
    grp, tp = ("yh", "core"), ("yl", "x")
    in_specs = (
        P(grp, "z", tp, None),
        P(grp, "z", None, tp),
        P(grp),
        P(grp, None),
        P(grp, None),
        P(),
        P(None, None, tp),
    )
    out_specs = P((*grp, "z"), tp)
    return jax.shard_map(
        make_body(seq_size), mesh=fine, in_specs=in_specs, out_specs=out_specs, check_vma=False
    )
```

time: 133 us -> 126 us (0.947)
  the two profiles are of different devices: /device:TPU:8 before, /device:TPU:6 now
where the time goes in v2:
time: 126 us; the launch traced here: 125 us
  blocking collectives  44.1 us (35%)
  starting transfers between devices  44 us (35%)
  waiting for transfers between devices  19.2 us (15%)
  Pallas kernels  12.7 us (10%)
  other arithmetic  2.49 us (2%)
  local copies, waits for them, and re-layouts  1.94 us (2%)
    all_to_all x1, blocking collectives, step(): parts = lax.all_to_all(total.astype(jnp.bfloat16), 'z', 0, 0, tiled=True)  29.3 us
    ppermute x7, starting transfers between devices, step(): normed.append(lax.ppermute(local, tp, pairs))  23.4 us
    all_to_all x1, starting transfers between devices, step(): lax.all_to_all(dout[0, 0].reshape(seq_size, chunk, head_cols), 'z', 0, 0,...  15.2 us
    all_to_all x1, blocking collectives, step(): lax.all_to_all(total.astype(jnp.bfloat16).reshape(GRP_OUTER, -1, head_col...  14.8 us
    all_to_all x1, waiting for transfers between devices, step(): lax.all_to_all(dout[0, 0].reshape(seq_size, chunk, head_cols), 'z', 0, 0,...  12.2 us
    pallas_call x1, Pallas kernels, weight_partials(): pl.pallas_call(grads_kernel, out_shape=(jax.ShapeDtypeStruct(half, jnp.bf...  8.69 us
    ppermute x7, waiting for transfers between devices, step(): normed.append(lax.ppermute(local, tp, pairs))  5.15 us
    all_to_all x1, starting transfers between devices, step(): cotangent = lax.all_to_all(routed, 'z', 0, 0, tiled=True)  3.53 us
  transfers between devices with their start and end apart: 10, of which 4 were waited for; matrix products, arithmetic and copies ran while one was open for 1% of the time, Pallas kernels for 1%

profile of v2, /device:TPU:6, one launch (start us, length us, event | category | flops | bytes accessed | tf_op | source)
XLA Modules:
  0.0 125.4 jit_solution(3127416873099758053)
XLA Ops:
  0.0 15.2 %all-to-all-start = ((bf16[12,48,128]{2,1,0:T(8,128)(2,1)}), bf16[12,48,128]{2,1,0:T(8,128)(2,1)S(1)}, u32[]{:S(2)}, u32[]{:S(2)}) async-start(bf16[12,48,128]{2,1,0:T(8,128)(2,1)} %bitcast.7), calls=%async_computation | async-start | bytes 294912 | tf_op jit(solution)/shard_map/all_to_all | solution.py:159
  15.8 12.2 %all-to-all-done.pieces_hbm = bf16[12,48,128]{2,1,0:T(8,128)(2,1)S(1)} async-done(((bf16[12,48,128]{2,1,0:T(8,128)(2,1)}), bf16[12,48,128]{2,1,0:T(8,128)(2,1)S(1)}, u32[]{:S(2)}, u32[]{:S(2)}) %all-to-all-start) | async-done | bytes 147488 | tf_op jit(solution)/shard_map/all_to_all | solution.py:159
  28.0 0.7 copy-done.1
  28.7 2.3 %route.1 = bf16[12,48,128]{2,1,0:T(8,128)(2,1)} custom-call(s32[1]{0:T(128)S(6)} %copy.8.count_ref, s32[1,12]{1,0:T(1,128)} %ids_ref.1, s32[1,12]{1,0:T(1,128)} %slot_ref.1, bf16[12,48,128]{2,1,0:T(8,128)(2,1)} %copy-done.1), custom_call_target="tpu_custom_call" | custom-call | tf_op jit(solution)/shard_map/route/pallas_call | solution.py:56
  30.9 0.0 copy-start.9
  30.9 3.5 %all-to-all-start.1 = ((bf16[12,48,128]{2,1,0:T(8,128)(2,1)}), bf16[12,48,128]{2,1,0:T(8,128)(2,1)S(1)}, u32[]{:S(2)}, u32[]{:S(2)}) async-start(bf16[12,48,128]{2,1,0:T(8,128)(2,1)} %route.1), calls=%async_computation.1 | async-start | bytes 294912 | tf_op jit(solution)/shard_map/all_to_all | solution.py:163
  34.5 0.6 broadcast_in_dim.3.gain_ref
  35.1 1.8 %norm.1.refs_0_ = bf16[72,1024]{1,0:T(8,128)(2,1)} custom-call(bf16[72,1024]{1,0:T(8,128)(2,1)} %bitcast.8, bf16[1,1024]{1,0:T(2,128)(2,1)} %broadcast_in_dim.3.gain_ref), custom_call_target="tpu_custom_call" | custom-call | tf_op jit(solution)/shard_map/norm/pallas_call | solution.py:34
  36.9 3.4 %collective-permute-start.6 = (bf16[72,1024]{1,0:T(8,128)(2,1)}, bf16[72,1024]{1,0:T(8,128)(2,1)S(1)}, u32[]{:S(2)}, u32[]{:S(2)}) collective-permute-start(bf16[72,1024]{1,0:T(8,128)(2,1)} %norm.1.refs_0_), channel_id=1, source_target_pairs={{0,12},{12,24},{24,36},{36,48},{48,60},{60,72},{72,84},{84,0},{1,1... | collective-permute-start | bytes 442376 | tf_op jit(solution)/shard_map/ppermute | solution.py:171
  40.3 4.3 %collective-permute-start.5 = (bf16[72,1024]{1,0:T(8,128)(2,1)}, bf16[72,1024]{1,0:T(8,128)(2,1)S(1)}, u32[]{:S(2)}, u32[]{:S(2)}) collective-permute-start(bf16[72,1024]{1,0:T(8,128)(2,1)} %norm.1.refs_0_), channel_id=1, source_target_pairs={{0,24},{12,36},{24,48},{36,60},{48,72},{60,84},{72,0},{84,12},{1,2... | collective-permute-start | bytes 442376 | tf_op jit(solution)/shard_map/ppermute | solution.py:171
  44.6 1.9 %collective-permute-start.4 = (bf16[72,1024]{1,0:T(8,128)(2,1)}, bf16[72,1024]{1,0:T(8,128)(2,1)S(1)}, u32[]{:S(2)}, u32[]{:S(2)}) collective-permute-start(bf16[72,1024]{1,0:T(8,128)(2,1)} %norm.1.refs_0_), channel_id=1, source_target_pairs={{0,36},{12,48},{24,60},{36,72},{48,84},{60,0},{72,12},{84,24},{1,3... | collective-permute-start | bytes 442376 | tf_op jit(solution)/shard_map/ppermute | solution.py:171
  46.5 3.3 %collective-permute-start.3 = (bf16[72,1024]{1,0:T(8,128)(2,1)}, bf16[72,1024]{1,0:T(8,128)(2,1)S(1)}, u32[]{:S(2)}, u32[]{:S(2)}) collective-permute-start(bf16[72,1024]{1,0:T(8,128)(2,1)} %norm.1.refs_0_), channel_id=1, source_target_pairs={{0,48},{12,60},{24,72},{36,84},{48,0},{60,12},{72,24},{84,36},{1,4... | collective-permute-start | bytes 442376 | tf_op jit(solution)/shard_map/ppermute | solution.py:171
  49.8 4.2 %collective-permute-start.2 = (bf16[72,1024]{1,0:T(8,128)(2,1)}, bf16[72,1024]{1,0:T(8,128)(2,1)S(1)}, u32[]{:S(2)}, u32[]{:S(2)}) collective-permute-start(bf16[72,1024]{1,0:T(8,128)(2,1)} %norm.1.refs_0_), channel_id=1, source_target_pairs={{0,60},{12,72},{24,84},{36,0},{48,12},{60,24},{72,36},{84,48},{1,6... | collective-permute-start | bytes 442376 | tf_op jit(solution)/shard_map/ppermute | solution.py:171
  54.0 0.0 collective-permute-done.6.refs_7_
  54.1 2.7 %collective-permute-start.1 = (bf16[72,1024]{1,0:T(8,128)(2,1)}, bf16[72,1024]{1,0:T(8,128)(2,1)S(1)}, u32[]{:S(2)}, u32[]{:S(2)}) collective-permute-start(bf16[72,1024]{1,0:T(8,128)(2,1)} %norm.1.refs_0_), channel_id=1, source_target_pairs={{0,72},{12,84},{24,0},{36,12},{48,24},{60,36},{72,48},{84,60},{1,7... | collective-permute-start | bytes 442376 | tf_op jit(solution)/shard_map/ppermute | solution.py:171
  56.8 0.0 collective-permute-done.5.refs_6_
  56.8 3.6 %collective-permute-start = (bf16[72,1024]{1,0:T(8,128)(2,1)}, bf16[72,1024]{1,0:T(8,128)(2,1)S(1)}, u32[]{:S(2)}, u32[]{:S(2)}) collective-permute-start(bf16[72,1024]{1,0:T(8,128)(2,1)} %norm.1.refs_0_), channel_id=1, source_target_pairs={{0,84},{12,0},{24,12},{36,24},{48,36},{60,48},{72,60},{84,72},{1,8... | collective-permute-start | bytes 442376 | tf_op jit(solution)/shard_map/ppermute | solution.py:171
  60.4 0.6 pad_add_fusion.place_ref
  61.0 0.0 collective-permute-done.2.refs_3_
  61.0 3.1 %collective-permute-done.1.refs_2_ = bf16[72,1024]{1,0:T(8,128)(2,1)S(1)} collective-permute-done((bf16[72,1024]{1,0:T(8,128)(2,1)}, bf16[72,1024]{1,0:T(8,128)(2,1)S(1)}, u32[]{:S(2)}, u32[]{:S(2)}) %collective-permute-start.1) | collective-permute-done | bytes 147488 | tf_op jit(solution)/shard_map/ppermute | solution.py:171
  64.1 2.0 %collective-permute-done.refs_1_ = bf16[72,1024]{1,0:T(8,128)(2,1)S(1)} collective-permute-done((bf16[72,1024]{1,0:T(8,128)(2,1)}, bf16[72,1024]{1,0:T(8,128)(2,1)S(1)}, u32[]{:S(2)}, u32[]{:S(2)}) %collective-permute-start) | collective-permute-done | bytes 147488 | tf_op jit(solution)/shard_map/ppermute | solution.py:171
  66.1 0.0 all-to-all-done.1
  66.2 0.6 copy-done.8
  66.8 0.1 copy-done
  66.9 8.7 %grads.1 = (bf16[12,128,128]{2,1,0:T(8,128)(2,1)}, f32[12,128,128]{2,1,0:T(8,128)}) custom-call(s32[2]{0:T(128)} %pad_add_fusion.place_ref, bf16[72,1024]{1,0:T(8,128)(2,1)} %norm.1.refs_0_, bf16[72,1024]{1,0:T(8,128)(2,1)} %copy-done.8, bf16[72,1024]{1,0:T(8,128)(2,1)} %copy-done.7, bf16[72,1024]{1,0:T(8,128)(2,1)} %copy-done.6, ...), custom_call_target="tpu_custom_call" | custom-call | tf_op jit(solution)/shard_map/grads/pallas_call | solution.py:130
  75.6 1.9 %collective-permute-start.7 = (bf16[12,128,128]{2,1,0:T(8,128)(2,1)}, bf16[12,128,128]{2,1,0:T(8,128)(2,1)S(1)}, u32[]{:S(2)}, u32[]{:S(2)}) collective-permute-start(bf16[12,128,128]{2,1,0:T(8,128)(2,1)} %get-tuple-element.8), channel_id=1, source_target_pairs={{0,96},{96,0},{1,97},{97,1},{2,98},{98,2},{3,99},{99,3},{4,100},{1... | collective-permute-start | bytes 1179656 | tf_op jit(solution)/shard_map/ppermute | solution.py:176
  77.5 1.9 %collective-permute-done.7 = bf16[12,128,128]{2,1,0:T(8,128)(2,1)S(1)} collective-permute-done((bf16[12,128,128]{2,1,0:T(8,128)(2,1)}, bf16[12,128,128]{2,1,0:T(8,128)(2,1)S(1)}, u32[]{:S(2)}, u32[]{:S(2)}) %collective-permute-start.7) | collective-permute-done | bytes 393248 | tf_op jit(solution)/shard_map/ppermute | solution.py:176
  79.4 1.2 add_convert_fusion
  80.6 29.3 %all_to_all.20 = bf16[12,128,128]{2,1,0:T(8,128)(2,1)S(1)} all-to-all(bf16[12,128,128]{2,1,0:T(8,128)(2,1)S(1)} %add_convert_fusion), channel_id=1, replica_groups=mesh['yh'=4,'core'=2,'yl'=2,'x'=4,'z'=12] {'z'}, dimensions={0} | all-to-all | bytes 786432 | tf_op jit(solution)/shard_map/all_to_all | solution.py:178
  109.9 0.1 reduce_sum.21
  110.0 14.8 %all_to_all.21 = bf16[4,32,128]{2,1,0:T(8,128)(2,1)S(1)} all-to-all(bf16[4,32,128]{2,1,0:T(8,128)(2,1)S(1)} %bitcast.9), channel_id=1, replica_groups=mesh['yh'=4,'core'=2,'yl'=2,'x'=4,'z'=12] {'yh'}, dimensions={0} | all-to-all | bytes 65536 | tf_op jit(solution)/shard_map/all_to_all | solution.py:180
  124.8 0.6 convert_reduce_fusion
  (18 shorter events, 0.0 us)
Async XLA Ops:
  0.0 28.0 %all-to-all-start = ((bf16[12,48,128]{2,1,0:T(8,128)(2,1)}), bf16[12,48,128]{2,1,0:T(8,128)(2,1)S(1)}, u32[]{:S(2)}, u32[]{:S(2)}) async-start(bf16[12,48,128]{2,1,0:T(8,128)(2,1)} %bitcast.7), calls=%async_computation | async-start | bytes 294912 | tf_op jit(solution)/shard_map/all_to_all | solution.py:159
  28.0 0.7 copy-start.1
  30.9 3.6 %copy-start.9 = (bf16[1024]{0:T(1024)(128)(2,1)S(1)}, bf16[1024]{0:T(1024)(128)(2,1)}, u32[]{:S(2)}) copy-start(bf16[1024]{0:T(1024)(128)(2,1)} %param.12) | copy-start | bytes 6148
  30.9 35.2 %all-to-all-start.1 = ((bf16[12,48,128]{2,1,0:T(8,128)(2,1)}), bf16[12,48,128]{2,1,0:T(8,128)(2,1)S(1)}, u32[]{:S(2)}, u32[]{:S(2)}) async-start(bf16[12,48,128]{2,1,0:T(8,128)(2,1)} %route.1), calls=%async_computation.1 | async-start | bytes 294912 | tf_op jit(solution)/shard_map/all_to_all | solution.py:163
  36.9 17.2 %collective-permute-start.6 = (bf16[72,1024]{1,0:T(8,128)(2,1)}, bf16[72,1024]{1,0:T(8,128)(2,1)S(1)}, u32[]{:S(2)}, u32[]{:S(2)}) collective-permute-start(bf16[72,1024]{1,0:T(8,128)(2,1)} %norm.1.refs_0_), channel_id=1, source_target_pairs={{0,12},{12,24},{24,36},{36,48},{48,60},{60,72},{72,84},{84,0},{1,1... | collective-permute-start | bytes 442376 | tf_op jit(solution)/shard_map/ppermute | solution.py:171
  40.3 16.5 %collective-permute-start.5 = (bf16[72,1024]{1,0:T(8,128)(2,1)}, bf16[72,1024]{1,0:T(8,128)(2,1)S(1)}, u32[]{:S(2)}, u32[]{:S(2)}) collective-permute-start(bf16[72,1024]{1,0:T(8,128)(2,1)} %norm.1.refs_0_), channel_id=1, source_target_pairs={{0,24},{12,36},{24,48},{36,60},{48,72},{60,84},{72,0},{84,12},{1,2... | collective-permute-start | bytes 442376 | tf_op jit(solution)/shard_map/ppermute | solution.py:171
  44.6 16.4 %collective-permute-start.4 = (bf16[72,1024]{1,0:T(8,128)(2,1)}, bf16[72,1024]{1,0:T(8,128)(2,1)S(1)}, u32[]{:S(2)}, u32[]{:S(2)}) collective-permute-start(bf16[72,1024]{1,0:T(8,128)(2,1)} %norm.1.refs_0_), channel_id=1, source_target_pairs={{0,36},{12,48},{24,60},{36,72},{48,84},{60,0},{72,12},{84,24},{1,3... | collective-permute-start | bytes 442376 | tf_op jit(solution)/shard_map/ppermute | solution.py:171
  46.5 14.4 %collective-permute-start.3 = (bf16[72,1024]{1,0:T(8,128)(2,1)}, bf16[72,1024]{1,0:T(8,128)(2,1)S(1)}, u32[]{:S(2)}, u32[]{:S(2)}) collective-permute-start(bf16[72,1024]{1,0:T(8,128)(2,1)} %norm.1.refs_0_), channel_id=1, source_target_pairs={{0,48},{12,60},{24,72},{36,84},{48,0},{60,12},{72,24},{84,36},{1,4... | collective-permute-start | bytes 442376 | tf_op jit(solution)/shard_map/ppermute | solution.py:171
  49.8 11.2 %collective-permute-start.2 = (bf16[72,1024]{1,0:T(8,128)(2,1)}, bf16[72,1024]{1,0:T(8,128)(2,1)S(1)}, u32[]{:S(2)}, u32[]{:S(2)}) collective-permute-start(bf16[72,1024]{1,0:T(8,128)(2,1)} %norm.1.refs_0_), channel_id=1, source_target_pairs={{0,60},{12,72},{24,84},{36,0},{48,12},{60,24},{72,36},{84,48},{1,6... | collective-permute-start | bytes 442376 | tf_op jit(solution)/shard_map/ppermute | solution.py:171
  54.0 12.1 %copy-start.2 = (bf16[72,1024]{1,0:T(8,128)(2,1)}, bf16[72,1024]{1,0:T(8,128)(2,1)S(1)}, u32[]{:S(2)}) copy-start(bf16[72,1024]{1,0:T(8,128)(2,1)S(1)} %collective-permute-done.6.refs_7_) | copy-start | bytes 442372
  54.1 10.1 %collective-permute-start.1 = (bf16[72,1024]{1,0:T(8,128)(2,1)}, bf16[72,1024]{1,0:T(8,128)(2,1)S(1)}, u32[]{:S(2)}, u32[]{:S(2)}) collective-permute-start(bf16[72,1024]{1,0:T(8,128)(2,1)} %norm.1.refs_0_), channel_id=1, source_target_pairs={{0,72},{12,84},{24,0},{36,12},{48,24},{60,36},{72,48},{84,60},{1,7... | collective-permute-start | bytes 442376 | tf_op jit(solution)/shard_map/ppermute | solution.py:171
  56.8 9.4 %copy-start.3 = (bf16[72,1024]{1,0:T(8,128)(2,1)}, bf16[72,1024]{1,0:T(8,128)(2,1)S(1)}, u32[]{:S(2)}) copy-start(bf16[72,1024]{1,0:T(8,128)(2,1)S(1)} %collective-permute-done.5.refs_6_) | copy-start | bytes 442372
  56.8 9.4 %collective-permute-start = (bf16[72,1024]{1,0:T(8,128)(2,1)}, bf16[72,1024]{1,0:T(8,128)(2,1)S(1)}, u32[]{:S(2)}, u32[]{:S(2)}) collective-permute-start(bf16[72,1024]{1,0:T(8,128)(2,1)} %norm.1.refs_0_), channel_id=1, source_target_pairs={{0,84},{12,0},{24,12},{36,24},{48,36},{60,48},{72,60},{84,72},{1,8... | collective-permute-start | bytes 442376 | tf_op jit(solution)/shard_map/ppermute | solution.py:171
  61.0 5.2 %copy-start.4 = (bf16[72,1024]{1,0:T(8,128)(2,1)}, bf16[72,1024]{1,0:T(8,128)(2,1)S(1)}, u32[]{:S(2)}) copy-start(bf16[72,1024]{1,0:T(8,128)(2,1)S(1)} %collective-permute-done.4.refs_5_) | copy-start | bytes 442372
  61.0 5.2 %copy-start.5 = (bf16[72,1024]{1,0:T(8,128)(2,1)}, bf16[72,1024]{1,0:T(8,128)(2,1)S(1)}, u32[]{:S(2)}) copy-start(bf16[72,1024]{1,0:T(8,128)(2,1)S(1)} %collective-permute-done.3.refs_4_) | copy-start | bytes 442372
  61.0 5.2 %copy-start.6 = (bf16[72,1024]{1,0:T(8,128)(2,1)}, bf16[72,1024]{1,0:T(8,128)(2,1)S(1)}, u32[]{:S(2)}) copy-start(bf16[72,1024]{1,0:T(8,128)(2,1)S(1)} %collective-permute-done.2.refs_3_) | copy-start | bytes 442372
  64.1 2.1 %copy-start.7 = (bf16[72,1024]{1,0:T(8,128)(2,1)}, bf16[72,1024]{1,0:T(8,128)(2,1)S(1)}, u32[]{:S(2)}) copy-start(bf16[72,1024]{1,0:T(8,128)(2,1)S(1)} %collective-permute-done.1.refs_2_) | copy-start | bytes 442372
  66.1 0.7 copy-start.8
  66.2 0.7 copy-start
  75.6 3.8 %collective-permute-start.7 = (bf16[12,128,128]{2,1,0:T(8,128)(2,1)}, bf16[12,128,128]{2,1,0:T(8,128)(2,1)S(1)}, u32[]{:S(2)}, u32[]{:S(2)}) collective-permute-start(bf16[12,128,128]{2,1,0:T(8,128)(2,1)} %get-tuple-element.8), channel_id=1, source_target_pairs={{0,96},{96,0},{1,97},{97,1},{2,98},{98,2},{3,99},{99,3},{4,100},{1... | collective-permute-start | bytes 1179656 | tf_op jit(solution)/shard_map/ppermute | solution.py:176
